TPU v7x, 32 devices: a whole 2x2x4 slice. The times are simulated.
32 devices in a mesh: groups: 2 (over y), tile: 4 (over z), chan: 2 (over x), tm: 2 (over core).
Axes of the slice: x: 2, y: 2, z: 4, core: 2. Of those that a mesh axis runs over, the one named last changes fastest.
Arguments:
- latents: bfloat16 [8, 32, 576], P('tm', 'groups', 'tile'), parts along dimension 1, may hold values from -6 to 6
- tile_order: int32 [8], P('groups'), parts along dimension 0, may hold values from 0 to 3, each once
- w_in: bfloat16 [27, 16, 512], P(None, None, 'chan'), may hold values from -0.3125 to 0.3125
- gain_in: float32 [512], P('chan'), may hold values from 0.25 to 1.75
- shift_in: float32 [512], P('chan'), may hold values from -3 to 3
- w_mid: bfloat16 [27, 512, 512], P(None, None, 'chan'), may hold values from -0.0546875 to 0.0546875
- gain_mid: float32 [512], P('chan'), may hold values from 0.25 to 1.75
- shift_mid: float32 [512], P('chan'), may hold values from -3 to 3
- w_out: bfloat16 [3, 512], P(None, 'chan'), may hold values from -0.25 to 0.25
- blend_weight: float32 [8, 256], P('groups'), parts along dimension 0, may hold values from 0.25 to 4
Outputs:
- decoded: float32 [8, 6, 576], P('tm', 'groups', 'tile'), parts along dimension 1
There are 2 independent parts, one for each index of `groups`. A program takes and returns all parts, laid end to end along the dimension named above; an argument that names none is the same for every part. Nothing has to cross between parts.
Inputs may be any that keep to these rules, and one draw needn't show every extreme that they name: `tile_order`: each image block is held by exactly one latent block.
All inputs are finite; a program needn't handle non-finite values.
Results may differ from a plain program's by a relative error of at most 0.0037.
Values may be sent and summed in bfloat16 or wider, within the bound.
A program may use at most 64 MiB of HBM per device.

v0:
```python
import jax
import jax.numpy as jnp
from jax import lax
from jax.sharding import PartitionSpec as P

CH = 512
GROUPS = 32
TSIDE = 16
STRIDE = 12
GRID_X = 4
EPSILON = 1e-06


def shifted(value, axis, steps):
    count = lax.axis_size(axis)
    leading, last = (max(0, -steps), min(count, count - steps))
    return lax.ppermute(value, axis, [(source, source + steps) for source in range(leading, last)])


def window_index(tile_id, tiles):
    slots = jnp.arange(TSIDE * TSIDE, dtype=jnp.int32)
    row = tile_id // GRID_X * STRIDE + slots // TSIDE
    col = tile_id % GRID_X * STRIDE + slots % TSIDE
    valid = (row < tiles // GRID_X * STRIDE) & (col < GRID_X * STRIDE)
    block = row // STRIDE * GRID_X + col // STRIDE
    index = block * (STRIDE * STRIDE) + row % STRIDE * STRIDE + col % STRIDE
    return (jnp.where(valid, index, 0), valid)


def causal_conv(extended, weights, frames, side):
    pixels = side * side
    rows = jnp.arange(pixels, dtype=jnp.int32) // side
    cols = jnp.arange(pixels, dtype=jnp.int32) % side
    total = jnp.zeros((frames, weights.shape[2], pixels), jnp.float32)
    for depth in range(3):
        window = extended[depth : depth + frames]
        for down in range(3):
            for across in range(3):
                offset = (down - 1) * side + (across - 1)
                inside = (
                    (rows + down - 1 >= 0)
                    & (rows + down - 1 < side)
                    & (cols + across - 1 >= 0)
                    & (cols + across - 1 < side)
                )
                moved = jnp.roll(window, -offset, axis=2)
                moved = jnp.where(inside[None, None, :], moved, jnp.zeros_like(moved))
                total = total + jnp.einsum(
                    "fcp,co->fop",
                    moved,
                    weights[9 * depth + 3 * down + across],
                    preferred_element_type=jnp.float32,
                )
    return total


def with_history(values):
    frames = values.shape[0]
    earlier = shifted(values[frames - 2 :], "tm", 1)
    return jnp.concatenate([earlier, values], axis=0)


def normalize(values, gain, shift, total_frames):
    frames, chans, pixels = values.shape
    width = CH // GROUPS
    grouped = values.reshape(frames, chans // width, width, pixels)
    sums = jnp.sum(grouped, axis=(0, 2, 3))
    squares = jnp.sum(grouped * grouped, axis=(0, 2, 3))
    sums, squares = lax.psum((sums, squares), "tm")
    count = total_frames * width * pixels
    mean = sums / count
    variance = squares / count - mean * mean
    scale = lax.rsqrt(variance + EPSILON)
    normed = (grouped - mean[None, :, None, None]) * scale[None, :, None, None]
    normed = normed.reshape(frames, chans, pixels) * gain[None, :, None] + shift[None, :, None]
    return jax.nn.silu(normed).astype(jnp.bfloat16)


def spread(color, weight, index, total_pixels):
    numer = (
        jnp.zeros((color.shape[0], 3, total_pixels), jnp.float32)
        .at[:, :, index]
        .add(color * weight[None, None, :])
    )
    denom = jnp.zeros((total_pixels,), jnp.float32).at[index].add(weight)
    return (numer, denom)


def route_owned(numer, denom, tile_id, own):
    frames = numer.shape[0]
    margin = (GRID_X + 1) * own
    numer_wide = jnp.concatenate([numer, jnp.zeros((frames, 3, margin), jnp.float32)], axis=2)
    denom_wide = jnp.concatenate([denom, jnp.zeros((margin,), jnp.float32)], axis=0)
    first_pixel = tile_id * own

    def block_at(offset):
        start_pixel = first_pixel + offset * own
        return (
            lax.dynamic_slice_in_dim(numer_wide, start_pixel, own, 2),
            lax.dynamic_slice_in_dim(denom_wide, start_pixel, own, 0),
        )

    owned_numer, owned_denom = block_at(0)
    for offset in (1, GRID_X, GRID_X + 1):
        piece_numer, piece_denom = block_at(offset)
        got_numer, got_denom = shifted((piece_numer, piece_denom), "tile", offset)
        owned_numer = owned_numer + got_numer
        owned_denom = owned_denom + got_denom
    return (owned_numer, owned_denom)


def body(
    latents, tile_order, w_in, gain_in, shift_in, w_mid, gain_mid, shift_mid, w_out, blend_weight
):
    frames = latents.shape[0]
    total_frames = frames * lax.axis_size("tm")
    tiles = tile_order.shape[0]
    own = STRIDE * STRIDE
    total_pixels = tiles * own
    tile_id = lax.axis_index("tile")
    index, valid = window_index(tile_id, tiles)
    whole = lax.all_gather(latents, "tile", axis=2, tiled=True)
    blocks = whole.reshape(frames, whole.shape[1], tiles, own)
    image = (
        jnp.zeros_like(blocks)
        .at[:, :, tile_order]
        .set(blocks)
        .reshape(frames, whole.shape[1], total_pixels)
    )
    window = jnp.where(
        valid[None, None, :], jnp.take(image, index, axis=2), jnp.zeros((), jnp.bfloat16)
    )
    first = causal_conv(with_history(window), w_in, frames, TSIDE)
    hidden = normalize(first, gain_in, shift_in, total_frames)
    second = causal_conv(
        lax.all_gather(with_history(hidden), "chan", axis=1, tiled=True), w_mid, frames, TSIDE
    )
    upper = normalize(second, gain_mid, shift_mid, total_frames)
    color = jnp.einsum("oc,fcp->fop", w_out, upper, preferred_element_type=jnp.float32)
    weight = jnp.where(valid, blend_weight[tile_id], jnp.float32(0.0))
    numer, denom = spread(color, weight, index, total_pixels)
    numer, denom = route_owned(numer, denom, tile_id, own)
    numer = lax.psum(numer, "chan")
    return numer / denom[None, None, :]


def solution(mesh):
    placed = (
        P("tm", "groups", "tile"),
        P("groups"),
        P(None, None, "chan"),
        P("chan"),
        P("chan"),
        P(None, None, "chan"),
        P("chan"),
        P("chan"),
        P(None, "chan"),
        P("groups", None),
    )
    return jax.shard_map(
        body, mesh=mesh, in_specs=placed, out_specs=P("tm", "groups", "tile"), check_vma=False
    )
```

profile of v0, /device:TPU:0, one launch (start us, length us, event | category | flops | bytes accessed | tf_op | source)
XLA Modules:
  0.0 141.7 jit_solution(11770328538480830236)
XLA Ops:
  6.6 1.0 copy.204
  7.6 18.3 %all_gather.6 = bf16[4,16,576]{1,0,2:T(4,128)(2,1)S(1)} all-gather(bf16[4,16,144]{1,0,2:T(4,128)(2,1)S(1)} %copy.204), channel_id=1, replica_groups=mesh['groups'=2,'tile'=4,'chan'=2,'tm'=2] {'tile'}, dimensions={2}, use_global_device_ids=true | all-gather | bytes 92160 | tf_op jit(solution)/shard_map/all_gather | solution.py:122
  26.2 0.7 compare_select_fusion.2
  26.9 0.7 scatter_fusion
  27.9 1.0 gather_fusion
  29.1 1.3 collective-permute-start
  30.5 0.7 collective-permute-done
  43.4 2.5 %all-reduce.3 = (f32[16]{0:T(128)S(1)}, f32[16]{0:T(128)S(1)}) all-reduce(f32[16]{0:T(128)S(1)} %reduce_sum.54, f32[16]{0:T(128)S(1)} %reduce_sum.51), channel_id=1, replica_groups=mesh['groups'=2,'tile'=4,'chan'=2,'tm'=2] {'tm'}, use_global_device_ids=true, to_apply=%region_6.7 | all-reduce | flops 32 | bytes 256 | tf_op jit(solution)/shard_map/psum | solution.py:69
  46.6 2.3 %collective-permute-start.1 = (bf16[2,256,256]{1,2,0:T(8,128)(2,1)S(1)}, bf16[2,256,256]{1,2,0:T(8,128)(2,1)S(1)}, u32[]{:S(2)}, u32[]{:S(2)}) collective-permute-start(bf16[2,256,256]{1,2,0:T(8,128)(2,1)S(1)} %slice.825), channel_id=1, source_target_pairs={{0,1},{2,3},{4,5},{6,7},{8,9},{10,11},{12,13},{14,15},{16,17},{18,... | collective-permute-start | bytes 786440 | tf_op jit(solution)/shard_map/ppermute | solution.py:17
  48.9 1.1 collective-permute-done.1
  50.0 0.9 pad_maximum_fusion
  51.0 2.3 %scatter_custom_fusion.2 = f32[576]{0:T(1024)S(1)} fusion(s32[256]{0:T(256)S(1)} %bitcast.322, f32[256]{0:T(256)S(1)} %broadcast_select_fusion, f32[]{:T(128)} %constant.166.clone.1), kind=kCustom, calls=%fused_computation.579 | custom fusion | flops 256 | bytes 2308 | tf_op jit(solution)/shard_map/scatter-add | solution.py:85
  53.4 3.4 %collective-permute-start.5 = (f32[144]{0:T(256)S(1)}, f32[144]{0:T(256)S(1)}, u32[]{:S(2)}, u32[]{:S(2)}) collective-permute-start(f32[144]{0:T(256)S(1)} %get-tuple-element.115), channel_id=1, source_target_pairs={{0,4},{4,8},{8,12},{1,5},{5,9},{9,13},{2,6},{6,10},{10,14},{3,7},{... | collective-permute-start | bytes 1736 | tf_op jit(solution)/shard_map/ppermute | solution.py:17
  56.9 0.7 collective-permute-start.6
  57.5 0.8 collective-permute-start.7
  58.4 21.1 %all-gather.2.cloned.1.call-done = bf16[6,512,256]{1,2,0:T(8,128)(2,1)} async-done(((bf16[6,256,256]{1,2,0:T(8,128)(2,1)}), bf16[6,512,256]{1,2,0:T(8,128)(2,1)}) %all-gather.2.cloned.1.call-update) | async-done | bytes 1572880 | tf_op jit(solution)/shard_map/all_gather | solution.py:136
  79.5 4.2 %fusion.506 = (bf16[4,512,239]{1,2,0:T(8,128)(2,1)S(1)}, bf16[4,512,239]{1,2,0:T(8,128)(2,1)S(1)}, bf16[4,512,239]{1,2,0:T(8,128)(2,1)S(1)}, bf16[4,512,239]{1,2...) fusion(bf16[6,512,256]{1,2,0:T(8,128)(2,1)} %all-gather.2.cloned.1.call-done), kind=kLoop, calls=%fused_computation.741 | loop fusion | bytes 11747328 | tf_op jit(solution)/shard_map/jit(_roll_static)/slice | solution.py:46
  83.8 1.4 %fusion.23 = f32[4,256,256]{2,1,0:T(8,128)S(1)} fusion(bf16[4,512,239]{1,2,0:T(8,128)(2,1)S(1)} %get-tuple-element.30, bf16[4,512,17]{1,2,0:T(8,128)(2,1)S(1)} %get-tuple-element.36, pred[256]{0:T(512)(128)(4,1)S(1)} %and_and_fusion.8, bf16[27,512,256]{2,1,0:T(8,128)(2,1)} %param.15), kind=kOutput, calls=%fused_computation.84 | convolution fusion | flops 271056896 | bytes 2359552 | tf_op jit(solution)/shard_map/fcp,co->fop/dot_general | solution.py:48
  85.2 1.4 %convolution_bitcast_fusion.8 = f32[4,256,256]{1,2,0:T(8,128)S(1)} fusion(bf16[4,512,239]{1,2,0:T(8,128)(2,1)S(1)} %get-tuple-element.27, bf16[4,512,17]{1,2,0:T(8,128)(2,1)S(1)} %get-tuple-element.33, pred[256]{0:T(512)(128)(4,1)S(1)} %and_and_fusion.8, bf16[27,512,256]{2,1,0:T(8,128)(2,1)} %param.15), kind=kOutput, calls=%fused_computation.12 | convolution fusion | flops 271056896 | bytes 2359552 | tf_op jit(solution)/shard_map/fcp,co->fop/dot_general | solution.py:48
  86.7 0.7 fusion.508
  87.4 1.4 %convolution_bitcast_fusion.7 = f32[4,256,256]{1,2,0:T(8,128)S(1)} fusion(bf16[4,512,240]{1,2,0:T(8,128)(2,1)S(1)} %get-tuple-element.39, bf16[4,512,16]{1,2,0:T(8,128)(2,1)S(1)} %get-tuple-element.45, pred[256]{0:T(512)(128)(4,1)S(1)} %get-tuple-element.131, bf16[27,512,256]{2,1,0:T(8,128)(2,1)} %param.15), kind=kOutput, calls=%fused_computation.11 | convolution fusion | flops 271056896 | bytes 2359552 | tf_op jit(solution)/shard_map/fcp,co->fop/dot_general | solution.py:48
  88.8 0.7 fusion.510
  89.6 1.5 %convolution_bitcast_fusion.6 = f32[4,256,256]{1,2,0:T(8,128)S(1)} fusion(bf16[4,512,241]{1,2,0:T(8,128)(2,1)S(1)} %get-tuple-element.51, bf16[4,512,15]{1,2,0:T(8,128)(2,1)S(1)} %get-tuple-element.57, pred[256]{0:T(512)(128)(4,1)S(1)} %get-tuple-element.130, bf16[27,512,256]{2,1,0:T(8,128)(2,1)} %param.15), kind=kOutput, calls=%fused_computation.10 | convolution fusion | flops 271056896 | bytes 2359552 | tf_op jit(solution)/shard_map/fcp,co->fop/dot_general | solution.py:48
  91.0 0.8 fusion.504
  91.9 1.4 %convolution_bitcast_fusion.5 = f32[4,256,256]{1,2,0:T(8,128)S(1)} fusion(bf16[4,512,255]{1,2,0:T(8,128)(2,1)S(1)} %get-tuple-element.14, bf16[4,512,1]{1,2,0:T(2,128)(2,1)S(1)} %get-tuple-element.20, pred[256]{0:T(512)(128)(4,1)S(1)} %get-tuple-element.129, bf16[27,512,256]{2,1,0:T(8,128)(2,1)} %param.15), kind=kOutput, calls=%fused_computation.9 | convolution fusion | flops 271056896 | bytes 2359552 | tf_op jit(solution)/shard_map/fcp,co->fop/dot_general | solution.py:48
  93.4 1.6 %convolution_bitcast_fusion.2 = f32[4,256,256]{1,2,0:T(8,128)S(1)} fusion(bf16[4,512,15]{1,2,0:T(8,128)(2,1)S(1)} %get-tuple-element.56, bf16[4,512,241]{1,2,0:T(8,128)(2,1)S(1)} %get-tuple-element.50, pred[256]{0:T(512)(128)(4,1)S(1)} %get-tuple-element.126, bf16[27,512,256]{2,1,0:T(8,128)(2,1)} %param.15), kind=kOutput, calls=%fused_computation.6 | convolution fusion | flops 271056896 | bytes 2359552 | tf_op jit(solution)/shard_map/fcp,co->fop/dot_general | solution.py:48
  95.0 1.4 %convolution_bitcast_fusion.1 = f32[4,256,256]{1,2,0:T(8,128)S(1)} fusion(bf16[4,512,16]{1,2,0:T(8,128)(2,1)S(1)} %get-tuple-element.44, bf16[4,512,240]{1,2,0:T(8,128)(2,1)S(1)} %get-tuple-element.38, pred[256]{0:T(512)(128)(4,1)S(1)} %get-tuple-element.125, bf16[27,512,256]{2,1,0:T(8,128)(2,1)} %param.15), kind=kOutput, calls=%fused_computation.5 | convolution fusion | flops 271056896 | bytes 2359552 | tf_op jit(solution)/shard_map/fcp,co->fop/dot_general | solution.py:48
  96.4 1.6 %convolution_bitcast_fusion = f32[4,256,256]{1,2,0:T(8,128)S(1)} fusion(bf16[4,512,17]{1,2,0:T(8,128)(2,1)S(1)} %get-tuple-element.32, bf16[4,512,239]{1,2,0:T(8,128)(2,1)S(1)} %get-tuple-element.26, pred[256]{0:T(512)(128)(4,1)S(1)} %get-tuple-element.124, bf16[27,512,256]{2,1,0:T(8,128)(2,1)} %param.15), kind=kOutput, calls=%fused_computation.4 | convolution fusion | flops 271056896 | bytes 2359552 | tf_op jit(solution)/shard_map/fcp,co->fop/dot_general | solution.py:48
  98.0 1.5 %convolution_add_fusion.31 = f32[4,256,256]{2,1,0:T(8,128)S(1)} fusion(f32[4,256,256]{2,1,0:T(8,128)S(1)} %fusion.23, bf16[4,512,240]{1,2,0:T(8,128)(2,1)S(1)} %get-tuple-element.42, bf16[4,512,16]{1,2,0:T(8,128)(2,1)S(1)} %get-tuple-element.48, pred[256]{0:T(512)(128)(4,1)S(1)} %get-tuple-element.131, bf16[27,512,256]{2,1,0:T(8,128)(2,1)} %param.15), kind=kOutput, calls=%fused_computation.77 | convolution fusion | flops 271319040 | bytes 3408128 | tf_op jit(solution)/shard_map/fcp,co->fop/dot_general | solution.py:48
  99.5 0.5 convolution_add_fusion.30
  100.0 0.5 convolution_add_fusion.29
  102.0 0.5 convolution_add_fusion.25
  102.5 0.5 convolution_add_fusion.24
  103.0 0.5 convolution_add_fusion.23
  104.0 0.5 convolution_add_fusion.21
  104.5 0.5 convolution_add_fusion.20
  105.5 0.5 convolution_add_fusion.18
  106.0 0.7 convolution_add_fusion.17
  106.7 0.5 fusion.21
  107.7 0.6 fusion.16
  108.4 0.6 fusion.502
  109.4 2.5 %all-reduce.2 = (f32[16]{0:T(128)S(1)}, f32[16]{0:T(128)S(1)}) all-reduce(f32[16]{0:T(128)S(1)} %reduce_sum.75, f32[16]{0:T(128)S(1)} %reduce_sum.72), channel_id=1, replica_groups=mesh['groups'=2,'tile'=4,'chan'=2,'tm'=2] {'tm'}, use_global_device_ids=true, to_apply=%region_12.13 | all-reduce | flops 32 | bytes 256 | tf_op jit(solution)/shard_map/psum | solution.py:69
  113.1 8.5 %scatter_fusion.1 = f32[4,3,576]{1,0,2:T(4,128)S(1)} fusion(f32[4,3,576]{1,0,2:T(4,128)S(1)} %broadcast_in_dim.385, s32[256]{0:T(256)S(1)} %bitcast.323, f32[256,4,3]{2,1,0:T(4,128)S(1)} %copy.210), kind=kCustom, calls=%fused_computation.2 | custom fusion | flops 3072 | bytes 37888 | tf_op jit(solution)/shard_map/scatter-add | solution.py:83
  122.2 3.4 %collective-permute-start.2 = (f32[4,3,144]{2,0,1:T(4,128)S(1)}, f32[4,3,144]{2,0,1:T(4,128)S(1)}, u32[]{:S(2)}, u32[]{:S(2)}) collective-permute-start(f32[4,3,144]{2,0,1:T(4,128)S(1)} %get-tuple-element.112), channel_id=1, source_target_pairs={{0,4},{4,8},{8,12},{1,5},{5,9},{9,13},{2,6},{6,10},{10,14},{3,7},{... | collective-permute-start | bytes 20744 | tf_op jit(solution)/shard_map/ppermute | solution.py:17
  125.6 0.7 collective-permute-start.3
  126.2 0.7 collective-permute-start.4
  127.1 7.1 %psum.39 = f32[4,3,144]{2,0,1:T(4,128)S(1)} all-reduce(f32[4,3,144]{2,0,1:T(4,128)S(1)} %fusion.326), channel_id=1, replica_groups=mesh['groups'=2,'tile'=4,'chan'=2,'tm'=2] {'chan'}, use_global_device_ids=true, to_apply=%region_14.15 | all-reduce | flops 1728 | bytes 13824 | tf_op jit(solution)/shard_map/psum | solution.py:143
  134.2 0.6 broadcast_divide_fusion
  (120 shorter events, 19.1 us)
Async XLA Ops:
  6.5 44.4 %copy-start = (f32[4,256]{1,0:T(4,128)S(1)}, f32[4,256]{1,0:T(4,128)}, u32[]{:S(2)}) copy-start(f32[4,256]{1,0:T(4,128)} %param.19) | copy-start | bytes 12292
  6.5 24.9 %copy-start.3 = (bf16[27,16,256]{2,1,0:T(8,128)(2,1)S(1)}, bf16[27,16,256]{2,1,0:T(8,128)(2,1)}, u32[]{:S(2)}) copy-start(bf16[27,16,256]{2,1,0:T(8,128)(2,1)} %param.12) | copy-start | bytes 663556
  6.5 72.9 %all-gather.2.cloned.1.call-start = ((), (), s32[]{:S(2)}) async-start(), calls=%async_computation | async-start | bytes 2359296 | tf_op jit(solution)/shard_map/all_gather | solution.py:136
  29.1 2.1 %collective-permute-start = (bf16[2,16,256]{2,1,0:T(8,128)(2,1)S(1)}, bf16[2,16,256]{2,1,0:T(8,128)(2,1)S(1)}, u32[]{:S(2)}, u32[]{:S(2)}) collective-permute-start(bf16[2,16,256]{2,1,0:T(8,128)(2,1)S(1)} %slice.742), channel_id=1, source_target_pairs={{0,1},{2,3},{4,5},{6,7},{8,9},{10,11},{12,13},{14,15},{16,17},{18,... | collective-permute-start | bytes 49160 | tf_op jit(solution)/shard_map/ppermute | solution.py:17
  42.2 4.1 %copy-start.4 = (f32[256]{0:T(256)S(1)}, f32[256]{0:T(256)}, u32[]{:S(2)}) copy-start(f32[256]{0:T(256)} %param.14) | copy-start | bytes 3076
  42.2 4.0 %copy-start.5 = (f32[256]{0:T(256)S(1)}, f32[256]{0:T(256)}, u32[]{:S(2)}) copy-start(f32[256]{0:T(256)} %param.13) | copy-start | bytes 3076
  46.6 3.4 %collective-permute-start.1 = (bf16[2,256,256]{1,2,0:T(8,128)(2,1)S(1)}, bf16[2,256,256]{1,2,0:T(8,128)(2,1)S(1)}, u32[]{:S(2)}, u32[]{:S(2)}) collective-permute-start(bf16[2,256,256]{1,2,0:T(8,128)(2,1)S(1)} %slice.825), channel_id=1, source_target_pairs={{0,1},{2,3},{4,5},{6,7},{8,9},{10,11},{12,13},{14,15},{16,17},{18,... | collective-permute-start | bytes 786440 | tf_op jit(solution)/shard_map/ppermute | solution.py:17
  53.4 72.8 %collective-permute-start.5 = (f32[144]{0:T(256)S(1)}, f32[144]{0:T(256)S(1)}, u32[]{:S(2)}, u32[]{:S(2)}) collective-permute-start(f32[144]{0:T(256)S(1)} %get-tuple-element.115), channel_id=1, source_target_pairs={{0,4},{4,8},{8,12},{1,5},{5,9},{9,13},{2,6},{6,10},{10,14},{3,7},{... | collective-permute-start | bytes 1736 | tf_op jit(solution)/shard_map/ppermute | solution.py:17
  56.9 70.0 %collective-permute-start.6 = (f32[144]{0:T(256)S(1)}, f32[144]{0:T(256)S(1)}, u32[]{:S(2)}, u32[]{:S(2)}) collective-permute-start(f32[144]{0:T(256)S(1)} %get-tuple-element.116), channel_id=1, source_target_pairs={} | collective-permute-start | bytes 1736 | tf_op jit(solution)/shard_map/ppermute | solution.py:17
  57.5 69.4 %collective-permute-start.7 = (f32[144]{0:T(256)S(1)}, f32[144]{0:T(256)S(1)}, u32[]{:S(2)}, u32[]{:S(2)}) collective-permute-start(f32[144]{0:T(256)S(1)} %get-tuple-element.117), channel_id=1, source_target_pairs={} | collective-permute-start | bytes 1736 | tf_op jit(solution)/shard_map/ppermute | solution.py:17
  79.5 4.2 %copy-start.2 = (bf16[6,512,256]{1,2,0:T(8,128)(2,1)S(1)}, bf16[6,512,256]{1,2,0:T(8,128)(2,1)}, u32[]{:S(2)}) copy-start(bf16[6,512,256]{1,2,0:T(8,128)(2,1)} %all-gather.2.cloned.1.call-done) | copy-start | bytes 4718596
  93.4 6.1 %slice-start = ((s8[7077888]{0:T(1024)(128)(4,1)}), s8[4194304]{0:T(1024)(128)(4,1)S(1)}, s32[]{:S(2)}) async-start(s8[7077888]{0:T(1024)(128)(4,1)} %bitcast.319), calls=%async_computation.1 | async-start | bytes 8388608
  96.4 3.1 %slice-start.1 = ((s8[7077888]{0:T(1024)(128)(4,1)}), s8[2883584]{0:T(1024)(128)(4,1)S(1)}, s32[]{:S(2)}) async-start(s8[7077888]{0:T(1024)(128)(4,1)} %bitcast.319), calls=%async_computation.2 | async-start | bytes 5767168
  108.4 3.8 %copy-start.6 = (bf16[3,256]{1,0:T(4,128)(2,1)S(1)}, bf16[3,256]{1,0:T(4,128)(2,1)}, u32[]{:S(2)}) copy-start(bf16[3,256]{1,0:T(4,128)(2,1)} %param.18) | copy-start | bytes 4612
  108.4 3.8 %copy-start.7 = (f32[256]{0:T(256)S(1)}, f32[256]{0:T(256)}, u32[]{:S(2)}) copy-start(f32[256]{0:T(256)} %param.17) | copy-start | bytes 3076
  108.4 3.8 %copy-start.8 = (f32[256]{0:T(256)S(1)}, f32[256]{0:T(256)}, u32[]{:S(2)}) copy-start(f32[256]{0:T(256)} %param.16) | copy-start | bytes 3076
  112.7 22.2 %copy-start.1 = (f32[4,256]{1,0:T(4,128)S(1)}, f32[4,256]{1,0:T(4,128)}, u32[]{:S(2)}) copy-start(f32[4,256]{1,0:T(4,128)} %param.19) | copy-start | bytes 12292
  122.2 4.8 %collective-permute-start.2 = (f32[4,3,144]{2,0,1:T(4,128)S(1)}, f32[4,3,144]{2,0,1:T(4,128)S(1)}, u32[]{:S(2)}, u32[]{:S(2)}) collective-permute-start(f32[4,3,144]{2,0,1:T(4,128)S(1)} %get-tuple-element.112), channel_id=1, source_target_pairs={{0,4},{4,8},{8,12},{1,5},{5,9},{9,13},{2,6},{6,10},{10,14},{3,7},{... | collective-permute-start | bytes 20744 | tf_op jit(solution)/shard_map/ppermute | solution.py:17
  125.6 1.4 %collective-permute-start.3 = (f32[4,3,144]{2,0,1:T(4,128)S(1)}, f32[4,3,144]{2,0,1:T(4,128)S(1)}, u32[]{:S(2)}, u32[]{:S(2)}) collective-permute-start(f32[4,3,144]{2,0,1:T(4,128)S(1)} %get-tuple-element.113), channel_id=1, source_target_pairs={} | collective-permute-start | bytes 20744 | tf_op jit(solution)/shard_map/ppermute | solution.py:17
  126.2 0.8 collective-permute-start.4
Sparse Core Ops, SparseCore 0:
  51.1 28.3 all-gather.1
where the time goes:
time: 142 us
  matrix products  33.9 us (24%)
  blocking collectives  30.3 us (21%)
  waiting for transfers between devices  23 us (16%)
  other arithmetic  14.9 us (10%)
  between operations  14.3 us (10%)
  starting transfers between devices  13.2 us (9%)
  local copies, waits for them, and re-layouts  12.1 us (9%)
    dot_general x54, matrix products, causal_conv(): jnp.einsum('fcp,co->fop', moved, weights[9 * depth + 3 * down + across],...  33.5 us
    all_gather x1, waiting for transfers between devices, body(): lax.all_gather(with_history(hidden), 'chan', axis=1, tiled=True)  21.1 us
    all_gather x1, blocking collectives, body(): whole = lax.all_gather(latents, 'tile', axis=2, tiled=True)  18.3 us
    ppermute x8, starting transfers between devices, shifted(): lax.ppermute(value, axis, [(source, source + steps) for source in range(l...  13.2 us
    scatter-add x1, other arithmetic, spread(): numer = jnp.zeros((color.shape[0], 3, total_pixels), jnp.float32).at[:, :...  8.52 us
    psum x1, blocking collectives, body(): numer = lax.psum(numer, 'chan')  7.13 us
    slice x8, local copies, waits for them, and re-layouts, causal_conv(): moved = jnp.roll(window, -offset, axis=2)  6.55 us
    psum x2, blocking collectives, normalize(): sums, squares = lax.psum((sums, squares), 'tm')  4.95 us
  transfers between devices with their start and end apart: 9, of which 3 were waited for; matrix products, arithmetic and copies ran while one was open for 30% of the time, Pallas kernels for 0%

commit v1 on v0

--- a/solution.py
+++ b/solution.py
@@ -119,7 +119,35 @@
     total_pixels = tiles * own
     tile_id = lax.axis_index("tile")
     index, valid = window_index(tile_id, tiles)
-    whole = lax.all_gather(latents, "tile", axis=2, tiled=True)
+    everything = lax.axis_index("tile")
+    out_arr = lax.axis_size("tile")
+    ledger = []
+    d_next, p_next, x_new = (out_arr, everything, latents.shape[2])
+    t = 0
+    while t < d_next:
+        ledger.append((t, (t + 1) % d_next))
+        t += 1
+    leaves = []
+    t = 0
+    while t < d_next:
+        leaves.append((t, (t - 1) % d_next))
+        t += 1
+    whole = jnp.zeros((*latents.shape[:2], d_next * x_new, *latents.shape[2 + 1 :]), latents.dtype)
+    whole = lax.dynamic_update_slice_in_dim(whole, latents, p_next * x_new, axis=2)
+    fresh = d_next // 2
+    i0 = 1
+    later = x_now = latents
+    while i0 < fresh + 1:
+        later = lax.ppermute(later, axis_name="tile", perm=ledger)
+        whole = lax.dynamic_update_slice_in_dim(
+            whole, later, (p_next - i0) % d_next * x_new, axis=2
+        )
+        if i0 < d_next - fresh:
+            x_now = lax.ppermute(x_now, axis_name="tile", perm=leaves)
+            whole = lax.dynamic_update_slice_in_dim(
+                whole, x_now, (p_next + i0) % d_next * x_new, axis=2
+            )
+        i0 = i0 + 1
     blocks = whole.reshape(frames, whole.shape[1], tiles, own)
     image = (
         jnp.zeros_like(blocks)

time: 142 us -> 134 us (0.944)
  blocking collectives: 30.3 us -> 12.1 us
  waiting for transfers between devices: 23 us -> 27.2 us
  starting transfers between devices: 13.2 us -> 16.2 us
  local copies, waits for them, and re-layouts: 12.1 us -> 14.5 us
    all_gather x1 -> x0, blocking collectives: 18.3 us -> none  [body(): whole = lax.all_gather(latents, 'tile', axis=2, tiled=True)]
    ppermute x0 -> x3, starting transfers between devices: none -> 5.14 us  [the longest x2 3.05 us: body(): later = lax.ppermute(later, axis_name='tile', perm=ledger)]
    ppermute x0 -> x3, waiting for transfers between devices: none -> 4.26 us  [the longest x2 4.26 us: body(): later = lax.ppermute(later, axis_name='tile', perm=ledger)]
    dynamic_update_slice x0 -> x4, local copies, waits for them, and re-layouts: none -> 3.43 us  [the longest x2 1.56 us: body(): lax.dynamic_update_slice_in_dim(whole, later, (p_next - i0) % d_next * x_...]
    ppermute x8, starting transfers between devices: 13.2 us -> 11 us  [shifted(): lax.ppermute(value, axis, [(source, source + steps) for source in range(l...]
  transfers between devices with their start and end apart: 9 -> 12, of which waited for: 3 -> 5; matrix products, arithmetic and copies ran while one was open for 30% -> 35% of each run, Pallas kernels for 0% -> 0%
where the time goes in v1:
time: 134 us; the launch traced here: 133 us
  matrix products  33.9 us (25%)
  waiting for transfers between devices  27.2 us (20%)
  starting transfers between devices  16.2 us (12%)
  other arithmetic  14.9 us (11%)
  local copies, waits for them, and re-layouts  14.5 us (11%)
  between operations  14.4 us (11%)
  blocking collectives  12.1 us (9%)
    dot_general x54, matrix products, causal_conv(): jnp.einsum('fcp,co->fop', moved, weights[9 * depth + 3 * down + across],...  33.4 us
    all_gather x1, waiting for transfers between devices, body(): lax.all_gather(with_history(hidden), 'chan', axis=1, tiled=True)  21 us
    ppermute x8, starting transfers between devices, shifted(): lax.ppermute(value, axis, [(source, source + steps) for source in range(l...  11 us
    scatter-add x1, other arithmetic, spread(): numer = jnp.zeros((color.shape[0], 3, total_pixels), jnp.float32).at[:, :...  8.52 us
    psum x1, blocking collectives, body(): numer = lax.psum(numer, 'chan')  7.14 us
    slice x8, local copies, waits for them, and re-layouts, causal_conv(): moved = jnp.roll(window, -offset, axis=2)  6.7 us
    psum x2, blocking collectives, normalize(): sums, squares = lax.psum((sums, squares), 'tm')  4.96 us
    ppermute x2, waiting for transfers between devices, body(): later = lax.ppermute(later, axis_name='tile', perm=ledger)  4.26 us
  transfers between devices with their start and end apart: 12, of which 5 were waited for; matrix products, arithmetic and copies ran while one was open for 35% of the time, Pallas kernels for 0%

profile of v1, /device:TPU:0, one launch (start us, length us, event | category | flops | bytes accessed | tf_op | source)
XLA Modules:
  0.0 133.1 jit_solution(11375420098898952887)
XLA Ops:
  6.5 3.1 %collective-permute-start = (bf16[4,16,144]{2,1,0:T(8,128)(2,1)}, bf16[4,16,144]{2,1,0:T(8,128)(2,1)S(1)}, u32[]{:S(2)}, u32[]{:S(2)}) collective-permute-start(bf16[4,16,144]{2,1,0:T(8,128)(2,1)} %param.10), channel_id=1, source_target_pairs={{0,4},{4,8},{8,12},{12,0},{1,5},{5,9},{9,13},{13,1},{2,6},{6,10},{... | collective-permute-start | bytes 55304 | tf_op jit(solution)/shard_map/ppermute | solution.py:141
  9.6 2.1 %collective-permute-start.1 = (bf16[4,16,144]{2,1,0:T(8,128)(2,1)}, bf16[4,16,144]{2,1,0:T(8,128)(2,1)S(1)}, u32[]{:S(2)}, u32[]{:S(2)}) collective-permute-start(bf16[4,16,144]{2,1,0:T(8,128)(2,1)} %param.10), channel_id=1, source_target_pairs={{0,12},{4,0},{8,4},{12,8},{1,13},{5,1},{9,5},{13,9},{2,14},{6,2},{... | collective-permute-start | bytes 55304 | tf_op jit(solution)/shard_map/ppermute | solution.py:146
  11.8 0.7 compare_select_fusion.2
  12.5 1.4 %collective-permute-done = bf16[4,16,144]{2,1,0:T(8,128)(2,1)S(1)} collective-permute-done((bf16[4,16,144]{2,1,0:T(8,128)(2,1)}, bf16[4,16,144]{2,1,0:T(8,128)(2,1)S(1)}, u32[]{:S(2)}, u32[]{:S(2)}) %collective-permute-start) | collective-permute-done | bytes 18464 | tf_op jit(solution)/shard_map/ppermute | solution.py:141
  13.9 1.0 dynamic_update_slice.12
  14.9 0.8 dynamic_update_slice.13
  15.8 0.9 dynamic_update_slice.14
  16.7 2.9 %collective-permute-done.2 = bf16[4,16,144]{2,1,0:T(8,128)(2,1)S(1)} collective-permute-done((bf16[4,16,144]{2,1,0:T(8,128)(2,1)S(1)}, bf16[4,16,144]{2,1,0:T(8,128)(2,1)S(1)}, u32[]{:S(2)}, u32[]{:S(2)}) %collective-permute-start.2) | collective-permute-done | bytes 18464 | tf_op jit(solution)/shard_map/ppermute | solution.py:141
  19.5 0.7 dynamic_update_slice.15
  20.5 0.7 scatter_fusion
  21.5 1.0 gather_fusion
  22.7 1.3 collective-permute-start.3
  24.0 0.8 collective-permute-done.3
  37.0 2.5 %all-reduce.3 = (f32[16]{0:T(128)S(1)}, f32[16]{0:T(128)S(1)}) all-reduce(f32[16]{0:T(128)S(1)} %reduce_sum.54, f32[16]{0:T(128)S(1)} %reduce_sum.51), channel_id=1, replica_groups=mesh['groups'=2,'tile'=4,'chan'=2,'tm'=2] {'tm'}, use_global_device_ids=true, to_apply=%region_6.7 | all-reduce | flops 32 | bytes 256 | tf_op jit(solution)/shard_map/psum | solution.py:69
  40.2 2.3 %collective-permute-start.4 = (bf16[2,256,256]{1,2,0:T(8,128)(2,1)S(1)}, bf16[2,256,256]{1,2,0:T(8,128)(2,1)S(1)}, u32[]{:S(2)}, u32[]{:S(2)}) collective-permute-start(bf16[2,256,256]{1,2,0:T(8,128)(2,1)S(1)} %slice.825), channel_id=1, source_target_pairs={{0,1},{2,3},{4,5},{6,7},{8,9},{10,11},{12,13},{14,15},{16,17},{18,... | collective-permute-start | bytes 786440 | tf_op jit(solution)/shard_map/ppermute | solution.py:17
  42.4 1.1 collective-permute-done.4
  43.6 1.0 pad_maximum_fusion
  44.6 2.3 %scatter_custom_fusion.2 = f32[576]{0:T(1024)S(1)} fusion(s32[256]{0:T(256)S(1)} %bitcast.320, f32[256]{0:T(256)S(1)} %broadcast_select_fusion, f32[]{:T(128)} %constant.183.clone.1), kind=kCustom, calls=%fused_computation.579 | custom fusion | flops 256 | bytes 2308 | tf_op jit(solution)/shard_map/scatter-add | solution.py:85
  47.0 0.6 collective-permute-start.10
  47.7 1.3 collective-permute-start.8
  49.0 0.8 collective-permute-start.9
  49.8 21.0 %all-gather.2.cloned.1.call-done = bf16[6,512,256]{1,2,0:T(8,128)(2,1)} async-done(((bf16[6,256,256]{1,2,0:T(8,128)(2,1)}), bf16[6,512,256]{1,2,0:T(8,128)(2,1)}) %all-gather.2.cloned.1.call-update) | async-done | bytes 1572880 | tf_op jit(solution)/shard_map/all_gather | solution.py:164
  70.8 4.4 %fusion.506 = (bf16[4,512,239]{1,2,0:T(8,128)(2,1)S(1)}, bf16[4,512,239]{1,2,0:T(8,128)(2,1)S(1)}, bf16[4,512,239]{1,2,0:T(8,128)(2,1)S(1)}, bf16[4,512,239]{1,2...) fusion(bf16[6,512,256]{1,2,0:T(8,128)(2,1)} %all-gather.2.cloned.1.call-done), kind=kLoop, calls=%fused_computation.741 | loop fusion | bytes 11747328 | tf_op jit(solution)/shard_map/jit(_roll_static)/slice | solution.py:46
  75.2 1.4 %fusion.23 = f32[4,256,256]{2,1,0:T(8,128)S(1)} fusion(bf16[4,512,239]{1,2,0:T(8,128)(2,1)S(1)} %get-tuple-element.30, bf16[4,512,17]{1,2,0:T(8,128)(2,1)S(1)} %get-tuple-element.36, pred[256]{0:T(512)(128)(4,1)S(1)} %and_and_fusion.8, bf16[27,512,256]{2,1,0:T(8,128)(2,1)} %param.15), kind=kOutput, calls=%fused_computation.84 | convolution fusion | flops 271056896 | bytes 2359552 | tf_op jit(solution)/shard_map/fcp,co->fop/dot_general | solution.py:48
  76.7 1.4 %convolution_bitcast_fusion.8 = f32[4,256,256]{1,2,0:T(8,128)S(1)} fusion(bf16[4,512,239]{1,2,0:T(8,128)(2,1)S(1)} %get-tuple-element.27, bf16[4,512,17]{1,2,0:T(8,128)(2,1)S(1)} %get-tuple-element.33, pred[256]{0:T(512)(128)(4,1)S(1)} %and_and_fusion.8, bf16[27,512,256]{2,1,0:T(8,128)(2,1)} %param.15), kind=kOutput, calls=%fused_computation.12 | convolution fusion | flops 271056896 | bytes 2359552 | tf_op jit(solution)/shard_map/fcp,co->fop/dot_general | solution.py:48
  78.1 0.7 fusion.508
  78.8 1.4 %convolution_bitcast_fusion.7 = f32[4,256,256]{1,2,0:T(8,128)S(1)} fusion(bf16[4,512,240]{1,2,0:T(8,128)(2,1)S(1)} %get-tuple-element.39, bf16[4,512,16]{1,2,0:T(8,128)(2,1)S(1)} %get-tuple-element.45, pred[256]{0:T(512)(128)(4,1)S(1)} %get-tuple-element.131, bf16[27,512,256]{2,1,0:T(8,128)(2,1)} %param.15), kind=kOutput, calls=%fused_computation.11 | convolution fusion | flops 271056896 | bytes 2359552 | tf_op jit(solution)/shard_map/fcp,co->fop/dot_general | solution.py:48
  80.3 0.7 fusion.510
  81.0 1.4 %convolution_bitcast_fusion.6 = f32[4,256,256]{1,2,0:T(8,128)S(1)} fusion(bf16[4,512,241]{1,2,0:T(8,128)(2,1)S(1)} %get-tuple-element.51, bf16[4,512,15]{1,2,0:T(8,128)(2,1)S(1)} %get-tuple-element.57, pred[256]{0:T(512)(128)(4,1)S(1)} %get-tuple-element.130, bf16[27,512,256]{2,1,0:T(8,128)(2,1)} %param.15), kind=kOutput, calls=%fused_computation.10 | convolution fusion | flops 271056896 | bytes 2359552 | tf_op jit(solution)/shard_map/fcp,co->fop/dot_general | solution.py:48
  82.4 0.8 fusion.504
  83.3 1.5 %convolution_bitcast_fusion.5 = f32[4,256,256]{1,2,0:T(8,128)S(1)} fusion(bf16[4,512,255]{1,2,0:T(8,128)(2,1)S(1)} %get-tuple-element.14, bf16[4,512,1]{1,2,0:T(2,128)(2,1)S(1)} %get-tuple-element.20, pred[256]{0:T(512)(128)(4,1)S(1)} %get-tuple-element.129, bf16[27,512,256]{2,1,0:T(8,128)(2,1)} %param.15), kind=kOutput, calls=%fused_computation.9 | convolution fusion | flops 271056896 | bytes 2359552 | tf_op jit(solution)/shard_map/fcp,co->fop/dot_general | solution.py:48
  84.8 1.6 %convolution_bitcast_fusion.2 = f32[4,256,256]{1,2,0:T(8,128)S(1)} fusion(bf16[4,512,15]{1,2,0:T(8,128)(2,1)S(1)} %get-tuple-element.56, bf16[4,512,241]{1,2,0:T(8,128)(2,1)S(1)} %get-tuple-element.50, pred[256]{0:T(512)(128)(4,1)S(1)} %get-tuple-element.126, bf16[27,512,256]{2,1,0:T(8,128)(2,1)} %param.15), kind=kOutput, calls=%fused_computation.6 | convolution fusion | flops 271056896 | bytes 2359552 | tf_op jit(solution)/shard_map/fcp,co->fop/dot_general | solution.py:48
  86.4 1.4 %convolution_bitcast_fusion.1 = f32[4,256,256]{1,2,0:T(8,128)S(1)} fusion(bf16[4,512,16]{1,2,0:T(8,128)(2,1)S(1)} %get-tuple-element.44, bf16[4,512,240]{1,2,0:T(8,128)(2,1)S(1)} %get-tuple-element.38, pred[256]{0:T(512)(128)(4,1)S(1)} %get-tuple-element.125, bf16[27,512,256]{2,1,0:T(8,128)(2,1)} %param.15), kind=kOutput, calls=%fused_computation.5 | convolution fusion | flops 271056896 | bytes 2359552 | tf_op jit(solution)/shard_map/fcp,co->fop/dot_general | solution.py:48
  87.8 1.6 %convolution_bitcast_fusion = f32[4,256,256]{1,2,0:T(8,128)S(1)} fusion(bf16[4,512,17]{1,2,0:T(8,128)(2,1)S(1)} %get-tuple-element.32, bf16[4,512,239]{1,2,0:T(8,128)(2,1)S(1)} %get-tuple-element.26, pred[256]{0:T(512)(128)(4,1)S(1)} %get-tuple-element.124, bf16[27,512,256]{2,1,0:T(8,128)(2,1)} %param.15), kind=kOutput, calls=%fused_computation.4 | convolution fusion | flops 271056896 | bytes 2359552 | tf_op jit(solution)/shard_map/fcp,co->fop/dot_general | solution.py:48
  89.4 1.5 %convolution_add_fusion.31 = f32[4,256,256]{2,1,0:T(8,128)S(1)} fusion(f32[4,256,256]{2,1,0:T(8,128)S(1)} %fusion.23, bf16[4,512,240]{1,2,0:T(8,128)(2,1)S(1)} %get-tuple-element.42, bf16[4,512,16]{1,2,0:T(8,128)(2,1)S(1)} %get-tuple-element.48, pred[256]{0:T(512)(128)(4,1)S(1)} %get-tuple-element.131, bf16[27,512,256]{2,1,0:T(8,128)(2,1)} %param.15), kind=kOutput, calls=%fused_computation.77 | convolution fusion | flops 271319040 | bytes 3408128 | tf_op jit(solution)/shard_map/fcp,co->fop/dot_general | solution.py:48
  91.4 0.5 convolution_add_fusion.29
  95.4 0.5 convolution_add_fusion.21
  95.9 0.5 convolution_add_fusion.20
  97.4 0.7 convolution_add_fusion.17
  99.1 0.6 fusion.16
  99.8 0.6 fusion.502
  100.8 2.5 %all-reduce.2 = (f32[16]{0:T(128)S(1)}, f32[16]{0:T(128)S(1)}) all-reduce(f32[16]{0:T(128)S(1)} %reduce_sum.75, f32[16]{0:T(128)S(1)} %reduce_sum.72), channel_id=1, replica_groups=mesh['groups'=2,'tile'=4,'chan'=2,'tm'=2] {'tm'}, use_global_device_ids=true, to_apply=%region_12.13 | all-reduce | flops 32 | bytes 256 | tf_op jit(solution)/shard_map/psum | solution.py:69
  104.5 8.5 %scatter_fusion.1 = f32[4,3,576]{1,0,2:T(4,128)S(1)} fusion(f32[4,3,576]{1,0,2:T(4,128)S(1)} %broadcast_in_dim.388, s32[256]{0:T(256)S(1)} %bitcast.321, f32[256,4,3]{2,1,0:T(4,128)S(1)} %copy.206), kind=kCustom, calls=%fused_computation.2 | custom fusion | flops 3072 | bytes 37888 | tf_op jit(solution)/shard_map/scatter-add | solution.py:83
  113.6 3.4 %collective-permute-start.5 = (f32[4,3,144]{2,0,1:T(4,128)S(1)}, f32[4,3,144]{2,0,1:T(4,128)S(1)}, u32[]{:S(2)}, u32[]{:S(2)}) collective-permute-start(f32[4,3,144]{2,0,1:T(4,128)S(1)} %get-tuple-element.112), channel_id=1, source_target_pairs={{0,4},{4,8},{8,12},{1,5},{5,9},{9,13},{2,6},{6,10},{10,14},{3,7},{... | collective-permute-start | bytes 20744 | tf_op jit(solution)/shard_map/ppermute | solution.py:17
  117.0 0.7 collective-permute-start.6
  117.7 0.7 collective-permute-start.7
  118.5 7.1 %psum.39 = f32[4,3,144]{2,0,1:T(4,128)S(1)} all-reduce(f32[4,3,144]{2,0,1:T(4,128)S(1)} %fusion.326), channel_id=1, replica_groups=mesh['groups'=2,'tile'=4,'chan'=2,'tm'=2] {'chan'}, use_global_device_ids=true, to_apply=%region_14.15 | all-reduce | flops 1728 | bytes 13824 | tf_op jit(solution)/shard_map/psum | solution.py:171
  125.7 0.6 broadcast_divide_fusion
  (130 shorter events, 21.9 us)
Async XLA Ops:
  6.5 38.0 %copy-start = (f32[4,256]{1,0:T(4,128)S(1)}, f32[4,256]{1,0:T(4,128)}, u32[]{:S(2)}) copy-start(f32[4,256]{1,0:T(4,128)} %param.19) | copy-start | bytes 12292
  6.5 18.4 %copy-start.3 = (bf16[27,16,256]{2,1,0:T(8,128)(2,1)S(1)}, bf16[27,16,256]{2,1,0:T(8,128)(2,1)}, u32[]{:S(2)}) copy-start(bf16[27,16,256]{2,1,0:T(8,128)(2,1)} %param.12) | copy-start | bytes 663556
  6.5 64.2 %all-gather.2.cloned.1.call-start = ((), (), s32[]{:S(2)}) async-start(), calls=%async_computation | async-start | bytes 2359296 | tf_op jit(solution)/shard_map/all_gather | solution.py:164
  6.5 7.3 %collective-permute-start = (bf16[4,16,144]{2,1,0:T(8,128)(2,1)}, bf16[4,16,144]{2,1,0:T(8,128)(2,1)S(1)}, u32[]{:S(2)}, u32[]{:S(2)}) collective-permute-start(bf16[4,16,144]{2,1,0:T(8,128)(2,1)} %param.10), channel_id=1, source_target_pairs={{0,4},{4,8},{8,12},{12,0},{1,5},{5,9},{9,13},{13,1},{2,6},{6,10},{... | collective-permute-start | bytes 55304 | tf_op jit(solution)/shard_map/ppermute | solution.py:141
  9.6 6.2 %collective-permute-start.1 = (bf16[4,16,144]{2,1,0:T(8,128)(2,1)}, bf16[4,16,144]{2,1,0:T(8,128)(2,1)S(1)}, u32[]{:S(2)}, u32[]{:S(2)}) collective-permute-start(bf16[4,16,144]{2,1,0:T(8,128)(2,1)} %param.10), channel_id=1, source_target_pairs={{0,12},{4,0},{8,4},{12,8},{1,13},{5,1},{9,5},{13,9},{2,14},{6,2},{... | collective-permute-start | bytes 55304 | tf_op jit(solution)/shard_map/ppermute | solution.py:146
  13.8 5.7 %collective-permute-start.2 = (bf16[4,16,144]{2,1,0:T(8,128)(2,1)S(1)}, bf16[4,16,144]{2,1,0:T(8,128)(2,1)S(1)}, u32[]{:S(2)}, u32[]{:S(2)}) collective-permute-start(bf16[4,16,144]{2,1,0:T(8,128)(2,1)S(1)} %collective-permute-done), channel_id=1, source_target_pairs={{0,4},{4,8},{8,12},{12,0},{1,5},{5,9},{9,13},{13,1},{2,6},{6,10},{... | collective-permute-start | bytes 55304 | tf_op jit(solution)/shard_map/ppermute | solution.py:141
  22.7 2.1 %collective-permute-start.3 = (bf16[2,16,256]{2,1,0:T(8,128)(2,1)S(1)}, bf16[2,16,256]{2,1,0:T(8,128)(2,1)S(1)}, u32[]{:S(2)}, u32[]{:S(2)}) collective-permute-start(bf16[2,16,256]{2,1,0:T(8,128)(2,1)S(1)} %slice.742), channel_id=1, source_target_pairs={{0,1},{2,3},{4,5},{6,7},{8,9},{10,11},{12,13},{14,15},{16,17},{18,... | collective-permute-start | bytes 49160 | tf_op jit(solution)/shard_map/ppermute | solution.py:17
  35.7 4.1 %copy-start.4 = (f32[256]{0:T(256)S(1)}, f32[256]{0:T(256)}, u32[]{:S(2)}) copy-start(f32[256]{0:T(256)} %param.14) | copy-start | bytes 3076
  35.7 4.1 %copy-start.5 = (f32[256]{0:T(256)S(1)}, f32[256]{0:T(256)}, u32[]{:S(2)}) copy-start(f32[256]{0:T(256)} %param.13) | copy-start | bytes 3076
  40.2 3.4 %collective-permute-start.4 = (bf16[2,256,256]{1,2,0:T(8,128)(2,1)S(1)}, bf16[2,256,256]{1,2,0:T(8,128)(2,1)S(1)}, u32[]{:S(2)}, u32[]{:S(2)}) collective-permute-start(bf16[2,256,256]{1,2,0:T(8,128)(2,1)S(1)} %slice.825), channel_id=1, source_target_pairs={{0,1},{2,3},{4,5},{6,7},{8,9},{10,11},{12,13},{14,15},{16,17},{18,... | collective-permute-start | bytes 786440 | tf_op jit(solution)/shard_map/ppermute | solution.py:17
  47.0 70.7 %collective-permute-start.10 = (f32[144]{0:T(256)S(1)}, f32[144]{0:T(256)S(1)}, u32[]{:S(2)}, u32[]{:S(2)}) collective-permute-start(f32[144]{0:T(256)S(1)} %get-tuple-element.117), channel_id=1, source_target_pairs={} | collective-permute-start | bytes 1736 | tf_op jit(solution)/shard_map/ppermute | solution.py:17
  47.7 70.7 %collective-permute-start.8 = (f32[144]{0:T(256)S(1)}, f32[144]{0:T(256)S(1)}, u32[]{:S(2)}, u32[]{:S(2)}) collective-permute-start(f32[144]{0:T(256)S(1)} %get-tuple-element.115), channel_id=1, source_target_pairs={{0,4},{4,8},{8,12},{1,5},{5,9},{9,13},{2,6},{6,10},{10,14},{3,7},{... | collective-permute-start | bytes 1736 | tf_op jit(solution)/shard_map/ppermute | solution.py:17
  49.0 69.4 %collective-permute-start.9 = (f32[144]{0:T(256)S(1)}, f32[144]{0:T(256)S(1)}, u32[]{:S(2)}, u32[]{:S(2)}) collective-permute-start(f32[144]{0:T(256)S(1)} %get-tuple-element.116), channel_id=1, source_target_pairs={} | collective-permute-start | bytes 1736 | tf_op jit(solution)/shard_map/ppermute | solution.py:17
  70.8 4.4 %copy-start.2 = (bf16[6,512,256]{1,2,0:T(8,128)(2,1)S(1)}, bf16[6,512,256]{1,2,0:T(8,128)(2,1)}, u32[]{:S(2)}) copy-start(bf16[6,512,256]{1,2,0:T(8,128)(2,1)} %all-gather.2.cloned.1.call-done) | copy-start | bytes 4718596
  84.8 6.1 %slice-start = ((s8[7077888]{0:T(1024)(128)(4,1)}), s8[4194304]{0:T(1024)(128)(4,1)S(1)}, s32[]{:S(2)}) async-start(s8[7077888]{0:T(1024)(128)(4,1)} %bitcast.317), calls=%async_computation.1 | async-start | bytes 8388608
  87.8 3.1 %slice-start.1 = ((s8[7077888]{0:T(1024)(128)(4,1)}), s8[2883584]{0:T(1024)(128)(4,1)S(1)}, s32[]{:S(2)}) async-start(s8[7077888]{0:T(1024)(128)(4,1)} %bitcast.317), calls=%async_computation.2 | async-start | bytes 5767168
  99.8 3.8 %copy-start.6 = (bf16[3,256]{1,0:T(4,128)(2,1)S(1)}, bf16[3,256]{1,0:T(4,128)(2,1)}, u32[]{:S(2)}) copy-start(bf16[3,256]{1,0:T(4,128)(2,1)} %param.18) | copy-start | bytes 4612
  99.8 3.8 %copy-start.7 = (f32[256]{0:T(256)S(1)}, f32[256]{0:T(256)}, u32[]{:S(2)}) copy-start(f32[256]{0:T(256)} %param.17) | copy-start | bytes 3076
  99.8 3.8 %copy-start.8 = (f32[256]{0:T(256)S(1)}, f32[256]{0:T(256)}, u32[]{:S(2)}) copy-start(f32[256]{0:T(256)} %param.16) | copy-start | bytes 3076
  104.1 22.2 %copy-start.1 = (f32[4,256]{1,0:T(4,128)S(1)}, f32[4,256]{1,0:T(4,128)}, u32[]{:S(2)}) copy-start(f32[4,256]{1,0:T(4,128)} %param.19) | copy-start | bytes 12292
  113.6 4.8 %collective-permute-start.5 = (f32[4,3,144]{2,0,1:T(4,128)S(1)}, f32[4,3,144]{2,0,1:T(4,128)S(1)}, u32[]{:S(2)}, u32[]{:S(2)}) collective-permute-start(f32[4,3,144]{2,0,1:T(4,128)S(1)} %get-tuple-element.112), channel_id=1, source_target_pairs={{0,4},{4,8},{8,12},{1,5},{5,9},{9,13},{2,6},{6,10},{10,14},{3,7},{... | collective-permute-start | bytes 20744 | tf_op jit(solution)/shard_map/ppermute | solution.py:17
  117.0 1.4 %collective-permute-start.6 = (f32[4,3,144]{2,0,1:T(4,128)S(1)}, f32[4,3,144]{2,0,1:T(4,128)S(1)}, u32[]{:S(2)}, u32[]{:S(2)}) collective-permute-start(f32[4,3,144]{2,0,1:T(4,128)S(1)} %get-tuple-element.113), channel_id=1, source_target_pairs={} | collective-permute-start | bytes 20744 | tf_op jit(solution)/shard_map/ppermute | solution.py:17
  117.7 0.8 collective-permute-start.7
Sparse Core Ops, SparseCore 0:
  44.7 26.0 all-gather.1
